TPU v7x, 256 devices: a whole 4x4x8 slice. The times are simulated.
256 devices in a mesh: seq: 16 (over y, x), dp: 16 (over z, core).
Axes of the slice: x: 4, y: 4, z: 8, core: 2. Of those that a mesh axis runs over, the one named last changes fastest.
Arguments:
- queries: bfloat16 [128, 256, 4096], P(None, ('seq', 'dp')), may hold values from -8 to 8
- keys_in: bfloat16 [128, 256, 4096], P(None, ('seq', 'dp')), may hold values from -8 to 8
- values: bfloat16 [128, 256, 4096], P(None, ('seq', 'dp')), may hold values from -6 to 6
- grad_out: bfloat16 [10, 4096, 4096], P(None, ('seq', 'dp')), may hold values from -6 to 6
- doc_lengths: int32 [24], replicated, may hold values from 1 to 2560, as said below
- doc_group: int32 [24], replicated, may hold values from 0 to 15, as said below
Outputs:
- attended: bfloat16 [10, 4096, 4096], P(None, ('seq', 'dp'))
- grad_queries: bfloat16 [128, 256, 4096], P(None, ('seq', 'dp'))
- grad_keys: bfloat16 [128, 256, 4096], P(None, ('seq', 'dp'))
- grad_values: bfloat16 [128, 256, 4096], P(None, ('seq', 'dp'))
Inputs may be any that keep to these rules, and one draw needn't show every extreme that they name: `doc_lengths`: the documents lie one after another in the packed batch in index order and their lengths sum to 32768. The documents of one group are consecutive, groups in increasing order; every group holds a whole multiple of 256 tokens, at most 2560, and some group holds exactly that many. `doc_group`: never falls from one document to the next; every group takes at least one document.
All inputs are finite; a program needn't handle non-finite values.
Results may differ from a plain program's by a relative error of at most 0.02.
Values may be sent and summed in bfloat16 or wider, within the bound.
A program may use at most 64 MiB of HBM per device.

v0:
```python
import jax
import jax.numpy as jnp
import numpy as np
from jax import lax
from jax.sharding import PartitionSpec as P

HEAD = 128


NEGATIVE_FILL = -1e30


def group_tables(doc_lengths, doc_group, group_count, per_unit):
    doc_ends = jnp.cumsum(doc_lengths)
    member = (doc_group[:, None] == jnp.arange(group_count, dtype=jnp.int32)[None, :]).astype(
        jnp.int32
    )
    group_units = jnp.sum(member * doc_lengths[:, None], axis=0) // per_unit
    first_unit = jnp.cumsum(group_units) - group_units
    return (doc_ends, group_units, first_unit)


def attend_group(
    head_q, head_k, head_v, head_do, token_ids, doc_query, doc_key, row_live, block_rows
):
    row_count, head_count, head_dim = head_q.shape
    blocks = row_count // block_rows
    score_scale = head_dim ** (-0.5)
    later, earlier = np.tril_indices(blocks)
    query_block = jnp.asarray(later, dtype=jnp.int32)
    key_block = jnp.asarray(earlier, dtype=jnp.int32)
    pair_total = int(later.shape[0])
    block_docs = doc_query.reshape(blocks, block_rows)
    live_blocks = row_live.reshape(blocks, block_rows)
    lowest = jnp.min(jnp.where(live_blocks, block_docs, 1 << 30), axis=1)
    highest = jnp.max(jnp.where(live_blocks, block_docs, -1), axis=1)
    needed = (
        (highest[key_block] >= lowest[query_block])
        & (lowest[key_block] <= highest[key_block])
        & (lowest[query_block] <= highest[query_block])
    )

    def tile_scores(pair_index):
        q_start = query_block[pair_index] * block_rows
        k_start = key_block[pair_index] * block_rows
        q_rows = lax.dynamic_slice_in_dim(head_q, q_start, block_rows, 0)
        k_rows = lax.dynamic_slice_in_dim(head_k, k_start, block_rows, 0)
        same_doc = (
            lax.dynamic_slice_in_dim(doc_query, q_start, block_rows, 0)[:, None]
            == lax.dynamic_slice_in_dim(doc_key, k_start, block_rows, 0)[None, :]
        )
        earlier_key = (
            lax.dynamic_slice_in_dim(token_ids, k_start, block_rows, 0)[None, :]
            <= lax.dynamic_slice_in_dim(token_ids, q_start, block_rows, 0)[:, None]
        )
        scores = (
            jnp.einsum("qhe,khe->qhk", q_rows, k_rows, preferred_element_type=jnp.float32)
            * score_scale
        )
        return (q_start, k_start, q_rows, k_rows, scores, (same_doc & earlier_key)[:, None, :])

    def stats_step(pair_index, loop_state):

        def stats_compute(inner_state):
            row_top, row_total = inner_state
            q_start, k_start, q_rows, k_rows, scores, allowed = tile_scores(pair_index)
            old_top = lax.dynamic_slice_in_dim(row_top, q_start, block_rows, 0)
            old_total = lax.dynamic_slice_in_dim(row_total, q_start, block_rows, 0)
            new_top = jnp.maximum(
                old_top, jnp.max(jnp.where(allowed, scores, NEGATIVE_FILL), axis=2)
            )
            exp_terms = jnp.sum(
                jnp.where(allowed, jnp.exp(scores - new_top[:, :, None]), 0.0), axis=2
            )
            new_total = old_total * jnp.exp(old_top - new_top) + exp_terms
            return (
                lax.dynamic_update_slice_in_dim(row_top, new_top, q_start, 0),
                lax.dynamic_update_slice_in_dim(row_total, new_total, q_start, 0),
            )

        return lax.cond(needed[pair_index], stats_compute, lambda unchanged: unchanged, loop_state)

    start_state = (
        jnp.full((row_count, head_count), NEGATIVE_FILL, jnp.float32),
        jnp.zeros((row_count, head_count), jnp.float32),
    )
    row_top, row_total = lax.fori_loop(0, pair_total, stats_step, start_state)
    log_total = jnp.where(row_live[:, None], row_top + jnp.log(row_total), 0.0)

    def value_step(pair_index, accumulated):

        def value_compute(inner_state):
            q_start, k_start, q_rows, k_rows, scores, allowed = tile_scores(pair_index)
            row_log = lax.dynamic_slice_in_dim(log_total, q_start, block_rows, 0)
            weight = jnp.where(allowed, jnp.exp(scores - row_log[:, :, None]), 0.0).astype(
                jnp.bfloat16
            )
            v_rows = lax.dynamic_slice_in_dim(head_v, k_start, block_rows, 0)
            part_sum = jnp.einsum(
                "qhk,khe->qhe", weight, v_rows, preferred_element_type=jnp.float32
            )
            current = lax.dynamic_slice_in_dim(inner_state, q_start, block_rows, 0)
            return lax.dynamic_update_slice_in_dim(inner_state, current + part_sum, q_start, 0)

        return lax.cond(needed[pair_index], value_compute, lambda unchanged: unchanged, accumulated)

    accumulated = lax.fori_loop(
        0, pair_total, value_step, jnp.zeros((row_count, head_count, head_dim), jnp.float32)
    )
    attended = accumulated.astype(jnp.bfloat16)
    delta_all = jnp.sum(head_do.astype(jnp.float32) * attended.astype(jnp.float32), axis=2)

    def grad_step(pair_index, loop_state):

        def grad_compute(inner_state):
            grad_q, grad_k, grad_v = inner_state
            q_start, k_start, q_rows, k_rows, scores, allowed = tile_scores(pair_index)
            row_log = lax.dynamic_slice_in_dim(log_total, q_start, block_rows, 0)
            row_delta = lax.dynamic_slice_in_dim(delta_all, q_start, block_rows, 0)
            weight_full = jnp.where(allowed, jnp.exp(scores - row_log[:, :, None]), 0.0)
            do_rows = lax.dynamic_slice_in_dim(head_do, q_start, block_rows, 0)
            v_rows = lax.dynamic_slice_in_dim(head_v, k_start, block_rows, 0)
            grad_prob = jnp.einsum(
                "qhe,khe->qhk", do_rows, v_rows, preferred_element_type=jnp.float32
            )
            grad_score = (weight_full * (grad_prob - row_delta[:, :, None])).astype(jnp.bfloat16)
            add_values = jnp.einsum(
                "qhk,qhe->khe",
                weight_full.astype(jnp.bfloat16),
                do_rows,
                preferred_element_type=jnp.float32,
            )
            add_queries = jnp.einsum(
                "qhk,khe->qhe", grad_score, k_rows, preferred_element_type=jnp.float32
            )
            add_keys = jnp.einsum(
                "qhk,qhe->khe", grad_score, q_rows, preferred_element_type=jnp.float32
            )
            grad_q = lax.dynamic_update_slice_in_dim(
                grad_q,
                lax.dynamic_slice_in_dim(grad_q, q_start, block_rows, 0) + add_queries,
                q_start,
                0,
            )
            grad_k = lax.dynamic_update_slice_in_dim(
                grad_k,
                lax.dynamic_slice_in_dim(grad_k, k_start, block_rows, 0) + add_keys,
                k_start,
                0,
            )
            grad_v = lax.dynamic_update_slice_in_dim(
                grad_v,
                lax.dynamic_slice_in_dim(grad_v, k_start, block_rows, 0) + add_values,
                k_start,
                0,
            )
            return (grad_q, grad_k, grad_v)

        return lax.cond(needed[pair_index], grad_compute, lambda unchanged: unchanged, loop_state)

    zero_grads = jnp.zeros((row_count, head_count, head_dim), jnp.float32)
    grad_q, grad_k, grad_v = lax.fori_loop(
        0, pair_total, grad_step, (zero_grads, zero_grads, zero_grads)
    )
    return (
        attended,
        (grad_q * score_scale).astype(jnp.bfloat16),
        (grad_k * score_scale).astype(jnp.bfloat16),
        grad_v.astype(jnp.bfloat16),
    )


def to_groups(first_part, second_part, third_part):
    return (
        lax.all_to_all(first_part, "dp", split_axis=1, concat_axis=1, tiled=True),
        lax.all_to_all(second_part, "dp", split_axis=1, concat_axis=1, tiled=True),
        lax.all_to_all(third_part, "dp", split_axis=1, concat_axis=1, tiled=True),
    )


def to_heads(first_part, second_part, third_part, fourth_part):
    return (
        lax.all_to_all(first_part, "seq", split_axis=2, concat_axis=1, tiled=True),
        lax.all_to_all(second_part, "seq", split_axis=2, concat_axis=1, tiled=True),
        lax.all_to_all(third_part, "seq", split_axis=2, concat_axis=1, tiled=True),
        lax.all_to_all(fourth_part, "seq", split_axis=2, concat_axis=1, tiled=True),
    )


def from_heads(first_part, second_part, third_part, fourth_part):
    return (
        lax.all_to_all(first_part, "seq", split_axis=1, concat_axis=2, tiled=True),
        lax.all_to_all(second_part, "seq", split_axis=1, concat_axis=2, tiled=True),
        lax.all_to_all(third_part, "seq", split_axis=1, concat_axis=2, tiled=True),
        lax.all_to_all(fourth_part, "seq", split_axis=1, concat_axis=2, tiled=True),
    )


def to_packed(first_part, second_part, third_part):
    return (
        lax.all_to_all(first_part, "dp", split_axis=1, concat_axis=1, tiled=True),
        lax.all_to_all(second_part, "dp", split_axis=1, concat_axis=1, tiled=True),
        lax.all_to_all(third_part, "dp", split_axis=1, concat_axis=1, tiled=True),
    )


def body(queries, keys_in, values, grad_out, doc_lengths, doc_group):
    seq_count = lax.axis_size("seq")
    group_count = lax.axis_size("dp")
    devices = seq_count * group_count
    local_rows = queries.shape[0]
    features = queries.shape[2]
    head_dim = HEAD
    local_heads = features // (seq_count * head_dim)
    capacity = grad_out.shape[0]
    doc_ends, group_units, first_unit = group_tables(doc_lengths, doc_group, group_count, devices)
    slot_ids = jnp.arange(capacity, dtype=jnp.int32)[:, None]
    filled = slot_ids < group_units[None, :]
    source_row = jnp.where(filled, first_unit[None, :] + slot_ids, 0).reshape(-1)
    row_ids = jnp.arange(local_rows, dtype=jnp.int32)
    row_group = jnp.sum((first_unit + group_units)[None, :] <= row_ids[:, None], axis=1)
    row_first = jnp.sum(
        jnp.where(
            jnp.arange(group_count, dtype=jnp.int32)[None, :] == row_group[:, None],
            first_unit[None, :],
            0,
        ),
        axis=1,
    )
    target_row = (row_ids - row_first) * group_count + row_group

    def pack_rows(local):
        taken_rows = jnp.take(local, source_row, axis=0).reshape(
            (capacity, group_count) + local.shape[1:]
        )
        keep_mask = filled.reshape((capacity, group_count) + (1,) * (local.ndim - 1))
        return jnp.where(keep_mask, taken_rows, jnp.zeros((), local.dtype))

    def unpack_rows(balanced):
        flat_rows = balanced.reshape((capacity * group_count,) + balanced.shape[2:])
        return jnp.take(flat_rows, target_row, axis=0)

    head_shape = (seq_count, local_heads, head_dim)
    group_rows = capacity * group_count * seq_count
    flat_q = queries.reshape(local_rows, features)
    flat_k = keys_in.reshape(local_rows, features)
    flat_v = values.reshape(local_rows, features)
    cot_rows = grad_out.reshape((capacity * group_count, 1) + head_shape)
    moved_q, moved_k, moved_v = to_groups(pack_rows(flat_q), pack_rows(flat_k), pack_rows(flat_v))
    lead_shape = (capacity * group_count, 1) + head_shape
    head_q, head_k, head_v, head_do = to_heads(
        moved_q.reshape(lead_shape),
        moved_k.reshape(lead_shape),
        moved_v.reshape(lead_shape),
        cot_rows,
    )
    work_shape = (group_rows, local_heads, head_dim)
    head_q = head_q.reshape(work_shape)
    head_k = head_k.reshape(work_shape)
    head_v = head_v.reshape(work_shape)
    head_do = head_do.reshape(work_shape)
    group_index = lax.axis_index("dp")
    slot_axis = jnp.arange(capacity, dtype=jnp.int32)[:, None, None]
    data_axis = jnp.arange(group_count, dtype=jnp.int32)[None, :, None]
    seq_axis = jnp.arange(seq_count, dtype=jnp.int32)[None, None, :]
    token_ids = (
        (first_unit[group_index] + slot_axis) * devices + seq_axis * group_count + data_axis
    ).reshape(-1)
    row_live = jnp.broadcast_to(
        slot_axis < group_units[group_index], (capacity, group_count, seq_count)
    ).reshape(-1)
    doc_of = jnp.sum(doc_ends[None, :] <= token_ids[:, None], axis=1)
    doc_query = jnp.where(row_live, doc_of, -1)
    doc_key = jnp.where(row_live, doc_of, -2)
    divisors = [
        factor
        for factor in range(1, capacity + 1)
        if capacity % factor == 0 and factor * devices <= 512
    ]
    block_rows = divisors[-1] * devices
    attended, grad_q, grad_k, grad_v = attend_group(
        head_q, head_k, head_v, head_do, token_ids, doc_query, doc_key, row_live, block_rows
    )
    back_shape = (capacity * group_count, seq_count, 1, local_heads, head_dim)
    seq_out, seq_q, seq_k, seq_v = from_heads(
        attended.reshape(back_shape),
        grad_q.reshape(back_shape),
        grad_k.reshape(back_shape),
        grad_v.reshape(back_shape),
    )
    flat_shape = (capacity, group_count, features)
    home_q, home_k, home_v = to_packed(
        seq_q.reshape(flat_shape), seq_k.reshape(flat_shape), seq_v.reshape(flat_shape)
    )
    out_q = unpack_rows(home_q)
    out_k = unpack_rows(home_k)
    out_v = unpack_rows(home_v)
    packed_shape = (local_rows, 1, features)
    return (
        seq_out.reshape(capacity, group_count, features),
        out_q.reshape(packed_shape),
        out_k.reshape(packed_shape),
        out_v.reshape(packed_shape),
    )


def solution(mesh):
    return jax.shard_map(
        body,
        mesh=mesh,
        in_specs=(
            P(None, ("seq", "dp"), None),
            P(None, ("seq", "dp"), None),
            P(None, ("seq", "dp"), None),
            P(None, ("seq", "dp"), None),
            P(),
            P(),
        ),
        out_specs=(
            P(None, ("seq", "dp"), None),
            P(None, ("seq", "dp"), None),
            P(None, ("seq", "dp"), None),
            P(None, ("seq", "dp"), None),
        ),
        check_vma=False,
    )
```

profile of v0, /device:TPU:1, one launch (start us, length us, event | category | flops | bytes accessed | tf_op | source)
XLA Modules:
  0.0 1028.3 jit_solution(3317540687620245920)
XLA Ops:
  36.4 60.6 %all_to_all.102 = bf16[10,16,4096]{2,0,1:T(8,128)(2,1)} all-to-all(bf16[10,16,4096]{2,0,1:T(8,128)(2,1)} %get-tuple-element.1227), channel_id=1, replica_groups=mesh['seq'=16,'dp'=16] {'dp'}, dimensions={1} | all-to-all | bytes 2621440 | tf_op jit(solution)/shard_map/all_to_all | solution.py:176
  97.0 53.7 %all_to_all.103 = bf16[10,16,4096]{2,0,1:T(8,128)(2,1)} all-to-all(bf16[10,16,4096]{2,0,1:T(8,128)(2,1)S(1)} %get-tuple-element.1226), channel_id=1, replica_groups=mesh['seq'=16,'dp'=16] {'dp'}, dimensions={1} | all-to-all | bytes 2621440 | tf_op jit(solution)/shard_map/all_to_all | solution.py:175
  165.1 37.7 %all-to-all-done = bf16[10,16,4096]{2,0,1:T(8,128)(2,1)S(1)} async-done(((bf16[10,16,4096]{2,0,1:T(8,128)(2,1)}), bf16[10,16,4096]{2,0,1:T(8,128)(2,1)S(1)}, u32[]{:S(2)}, u32[]{:S(2)}) %all-to-all-start) | async-done | bytes 1310752 | tf_op jit(solution)/shard_map/all_to_all | solution.py:177
  269.4 117.6 %while.54 = (s32[]{:T(128)}, f32[2560,2]{0,1:T(2,128)S(1)}, f32[2560,2]{0,1:T(2,128)S(1)}, pred[15]{0:T(512)(128)(4,1)S(1)}, s32[2560]{0:T(1024)S(1)}, /*index=5...) while((s32[]{:T(128)}, f32[2560,2]{0,1:T(2,128)S(1)}, ...), condition=%wide.region_13.15_spmd.clone.clone, body=%wide.region_8.14_spmd.sunk.clone.clone.sunk | while | flops 138678800 | bytes 5712918 | solution.py:87
  393.6 130.8 %while.55 = (s32[]{:T(128)}, f32[2560,2,128]{0,2,1:T(8,128)}, pred[15]{0:T(512)(128)(4,1)S(1)}, bf16[2560,2,128]{0,2,1:T(8,128)(2,1)}, s32[2560]{0:T(1024)S(1)},...) while((s32[]{:T(128)}, f32[2560,2,128]{0,2,1:T(8,128)}, ...), condition=%wide.region_17.19_spmd.clone.clone, body=%wide.region_14.18_spmd.sunk.clone.clone.sunk | while | flops 271452672 | bytes 2450426 | solution.py:107
  531.5 229.7 %while.56 = (s32[]{:T(128)}, f32[2560,2,128]{0,2,1:T(8,128)}, f32[2560,2,128]{0,2,1:T(8,128)}, f32[2560,2,128]{0,2,1:T(8,128)S(1)}, pred[15]{0:T(512)(128)(4,1)S...) while((s32[]{:T(128)}, f32[2560,2,128]{0,2,1:T(8,128)}, ...), condition=%wide.region_22.24_spmd.clone.clone, body=%wide.region_19.23_spmd.sunk.clone.clone.sunk | while | flops 675940864 | bytes 15043730 | solution.py:162
  533.1 14.0 %conditional.17 = ((f32[2560,2,128]{0,2,1:T(8,128)}, f32[2560,2,128]{0,2,1:T(8,128)}, f32[2560,2,128]{0,2,1:T(8,128)S(1)})) conditional(s32[]{:T(128)} %bitcast.135, (f32[2560,2,128]{0,2,1:T(8,128)}, f32[2560,2,128]{0,2,1:T(8,128)}, f32[2560,2,128]{0,2,1:T(8,128)S(1)}) %tuple.202, (s32[]{:T(128)}, f32[2560,2,128]{0,2,1:T(8,128)}, ...), branch_computations={%region_20.21_spmd, %region_21.22_spmd.clone} | conditional | flops 675940864 | bytes 15033202 | solution.py:159
  548.4 14.1 %conditional.17 = ((f32[2560,2,128]{0,2,1:T(8,128)}, f32[2560,2,128]{0,2,1:T(8,128)}, f32[2560,2,128]{0,2,1:T(8,128)S(1)})) conditional(s32[]{:T(128)} %bitcast.135, (f32[2560,2,128]{0,2,1:T(8,128)}, f32[2560,2,128]{0,2,1:T(8,128)}, f32[2560,2,128]{0,2,1:T(8,128)S(1)}) %tuple.202, (s32[]{:T(128)}, f32[2560,2,128]{0,2,1:T(8,128)}, ...), branch_computations={%region_20.21_spmd, %region_21.22_spmd.clone} | conditional | flops 675940864 | bytes 15033202 | solution.py:159
  563.7 14.0 %conditional.17 = ((f32[2560,2,128]{0,2,1:T(8,128)}, f32[2560,2,128]{0,2,1:T(8,128)}, f32[2560,2,128]{0,2,1:T(8,128)S(1)})) conditional(s32[]{:T(128)} %bitcast.135, (f32[2560,2,128]{0,2,1:T(8,128)}, f32[2560,2,128]{0,2,1:T(8,128)}, f32[2560,2,128]{0,2,1:T(8,128)S(1)}) %tuple.202, (s32[]{:T(128)}, f32[2560,2,128]{0,2,1:T(8,128)}, ...), branch_computations={%region_20.21_spmd, %region_21.22_spmd.clone} | conditional | flops 675940864 | bytes 15033202 | solution.py:159
  579.0 14.0 %conditional.17 = ((f32[2560,2,128]{0,2,1:T(8,128)}, f32[2560,2,128]{0,2,1:T(8,128)}, f32[2560,2,128]{0,2,1:T(8,128)S(1)})) conditional(s32[]{:T(128)} %bitcast.135, (f32[2560,2,128]{0,2,1:T(8,128)}, f32[2560,2,128]{0,2,1:T(8,128)}, f32[2560,2,128]{0,2,1:T(8,128)S(1)}) %tuple.202, (s32[]{:T(128)}, f32[2560,2,128]{0,2,1:T(8,128)}, ...), branch_computations={%region_20.21_spmd, %region_21.22_spmd.clone} | conditional | flops 675940864 | bytes 15033202 | solution.py:159
  594.3 14.0 %conditional.17 = ((f32[2560,2,128]{0,2,1:T(8,128)}, f32[2560,2,128]{0,2,1:T(8,128)}, f32[2560,2,128]{0,2,1:T(8,128)S(1)})) conditional(s32[]{:T(128)} %bitcast.135, (f32[2560,2,128]{0,2,1:T(8,128)}, f32[2560,2,128]{0,2,1:T(8,128)}, f32[2560,2,128]{0,2,1:T(8,128)S(1)}) %tuple.202, (s32[]{:T(128)}, f32[2560,2,128]{0,2,1:T(8,128)}, ...), branch_computations={%region_20.21_spmd, %region_21.22_spmd.clone} | conditional | flops 675940864 | bytes 15033202 | solution.py:159
  609.6 14.0 %conditional.17 = ((f32[2560,2,128]{0,2,1:T(8,128)}, f32[2560,2,128]{0,2,1:T(8,128)}, f32[2560,2,128]{0,2,1:T(8,128)S(1)})) conditional(s32[]{:T(128)} %bitcast.135, (f32[2560,2,128]{0,2,1:T(8,128)}, f32[2560,2,128]{0,2,1:T(8,128)}, f32[2560,2,128]{0,2,1:T(8,128)S(1)}) %tuple.202, (s32[]{:T(128)}, f32[2560,2,128]{0,2,1:T(8,128)}, ...), branch_computations={%region_20.21_spmd, %region_21.22_spmd.clone} | conditional | flops 675940864 | bytes 15033202 | solution.py:159
  624.9 14.0 %conditional.17 = ((f32[2560,2,128]{0,2,1:T(8,128)}, f32[2560,2,128]{0,2,1:T(8,128)}, f32[2560,2,128]{0,2,1:T(8,128)S(1)})) conditional(s32[]{:T(128)} %bitcast.135, (f32[2560,2,128]{0,2,1:T(8,128)}, f32[2560,2,128]{0,2,1:T(8,128)}, f32[2560,2,128]{0,2,1:T(8,128)S(1)}) %tuple.202, (s32[]{:T(128)}, f32[2560,2,128]{0,2,1:T(8,128)}, ...), branch_computations={%region_20.21_spmd, %region_21.22_spmd.clone} | conditional | flops 675940864 | bytes 15033202 | solution.py:159
  655.4 14.0 %conditional.17 = ((f32[2560,2,128]{0,2,1:T(8,128)}, f32[2560,2,128]{0,2,1:T(8,128)}, f32[2560,2,128]{0,2,1:T(8,128)S(1)})) conditional(s32[]{:T(128)} %bitcast.135, (f32[2560,2,128]{0,2,1:T(8,128)}, f32[2560,2,128]{0,2,1:T(8,128)}, f32[2560,2,128]{0,2,1:T(8,128)S(1)}) %tuple.202, (s32[]{:T(128)}, f32[2560,2,128]{0,2,1:T(8,128)}, ...), branch_computations={%region_20.21_spmd, %region_21.22_spmd.clone} | conditional | flops 675940864 | bytes 15033202 | solution.py:159
  670.6 14.0 %conditional.17 = ((f32[2560,2,128]{0,2,1:T(8,128)}, f32[2560,2,128]{0,2,1:T(8,128)}, f32[2560,2,128]{0,2,1:T(8,128)S(1)})) conditional(s32[]{:T(128)} %bitcast.135, (f32[2560,2,128]{0,2,1:T(8,128)}, f32[2560,2,128]{0,2,1:T(8,128)}, f32[2560,2,128]{0,2,1:T(8,128)S(1)}) %tuple.202, (s32[]{:T(128)}, f32[2560,2,128]{0,2,1:T(8,128)}, ...), branch_computations={%region_20.21_spmd, %region_21.22_spmd.clone} | conditional | flops 675940864 | bytes 15033202 | solution.py:159
  686.0 14.0 %conditional.17 = ((f32[2560,2,128]{0,2,1:T(8,128)}, f32[2560,2,128]{0,2,1:T(8,128)}, f32[2560,2,128]{0,2,1:T(8,128)S(1)})) conditional(s32[]{:T(128)} %bitcast.135, (f32[2560,2,128]{0,2,1:T(8,128)}, f32[2560,2,128]{0,2,1:T(8,128)}, f32[2560,2,128]{0,2,1:T(8,128)S(1)}) %tuple.202, (s32[]{:T(128)}, f32[2560,2,128]{0,2,1:T(8,128)}, ...), branch_computations={%region_20.21_spmd, %region_21.22_spmd.clone} | conditional | flops 675940864 | bytes 15033202 | solution.py:159
  701.2 14.0 %conditional.17 = ((f32[2560,2,128]{0,2,1:T(8,128)}, f32[2560,2,128]{0,2,1:T(8,128)}, f32[2560,2,128]{0,2,1:T(8,128)S(1)})) conditional(s32[]{:T(128)} %bitcast.135, (f32[2560,2,128]{0,2,1:T(8,128)}, f32[2560,2,128]{0,2,1:T(8,128)}, f32[2560,2,128]{0,2,1:T(8,128)S(1)}) %tuple.202, (s32[]{:T(128)}, f32[2560,2,128]{0,2,1:T(8,128)}, ...), branch_computations={%region_20.21_spmd, %region_21.22_spmd.clone} | conditional | flops 675940864 | bytes 15033202 | solution.py:159
  716.5 14.0 %conditional.17 = ((f32[2560,2,128]{0,2,1:T(8,128)}, f32[2560,2,128]{0,2,1:T(8,128)}, f32[2560,2,128]{0,2,1:T(8,128)S(1)})) conditional(s32[]{:T(128)} %bitcast.135, (f32[2560,2,128]{0,2,1:T(8,128)}, f32[2560,2,128]{0,2,1:T(8,128)}, f32[2560,2,128]{0,2,1:T(8,128)S(1)}) %tuple.202, (s32[]{:T(128)}, f32[2560,2,128]{0,2,1:T(8,128)}, ...), branch_computations={%region_20.21_spmd, %region_21.22_spmd.clone} | conditional | flops 675940864 | bytes 15033202 | solution.py:159
  731.8 14.1 %conditional.17 = ((f32[2560,2,128]{0,2,1:T(8,128)}, f32[2560,2,128]{0,2,1:T(8,128)}, f32[2560,2,128]{0,2,1:T(8,128)S(1)})) conditional(s32[]{:T(128)} %bitcast.135, (f32[2560,2,128]{0,2,1:T(8,128)}, f32[2560,2,128]{0,2,1:T(8,128)}, f32[2560,2,128]{0,2,1:T(8,128)S(1)}) %tuple.202, (s32[]{:T(128)}, f32[2560,2,128]{0,2,1:T(8,128)}, ...), branch_computations={%region_20.21_spmd, %region_21.22_spmd.clone} | conditional | flops 675940864 | bytes 15033202 | solution.py:159
  747.1 14.0 %conditional.17 = ((f32[2560,2,128]{0,2,1:T(8,128)}, f32[2560,2,128]{0,2,1:T(8,128)}, f32[2560,2,128]{0,2,1:T(8,128)S(1)})) conditional(s32[]{:T(128)} %bitcast.135, (f32[2560,2,128]{0,2,1:T(8,128)}, f32[2560,2,128]{0,2,1:T(8,128)}, f32[2560,2,128]{0,2,1:T(8,128)S(1)}) %tuple.202, (s32[]{:T(128)}, f32[2560,2,128]{0,2,1:T(8,128)}, ...), branch_computations={%region_20.21_spmd, %region_21.22_spmd.clone} | conditional | flops 675940864 | bytes 15033202 | solution.py:159
  843.7 19.6 %all-to-all-start.9 = ((bf16[10,16,4096]{2,0,1:T(8,128)(2,1)}), bf16[10,16,4096]{2,0,1:T(8,128)(2,1)S(1)}, u32[]{:S(2)}, u32[]{:S(2)}) async-start(bf16[10,16,4096]{2,0,1:T(8,128)(2,1)} %copy.177), calls=%async_computation.9 | async-start | bytes 4194304 | tf_op jit(solution)/shard_map/all_to_all | solution.py:201
  874.4 37.7 %all-to-all-done.9 = bf16[10,16,4096]{2,0,1:T(8,128)(2,1)S(1)} async-done(((bf16[10,16,4096]{2,0,1:T(8,128)(2,1)}), bf16[10,16,4096]{2,0,1:T(8,128)(2,1)S(1)}, u32[]{:S(2)}, u32[]{:S(2)}) %all-to-all-start.9) | async-done | bytes 1310752 | tf_op jit(solution)/shard_map/all_to_all | solution.py:201
  928.3 37.9 %all-to-all-done.11 = bf16[10,16,4096]{2,0,1:T(8,128)(2,1)} async-done(((bf16[10,16,4096]{2,0,1:T(8,128)(2,1)}), bf16[10,16,4096]{2,0,1:T(8,128)(2,1)}, u32[]{:S(2)}, u32[]{:S(2)}) %all-to-all-start.11) | async-done | bytes 1310752 | tf_op jit(solution)/shard_map/all_to_all | solution.py:202
  983.4 37.0 %all-to-all-done.13 = bf16[10,16,4096]{2,0,1:T(8,128)(2,1)} async-done(((bf16[10,16,4096]{2,0,1:T(8,128)(2,1)}), bf16[10,16,4096]{2,0,1:T(8,128)(2,1)}, u32[]{:S(2)}, u32[]{:S(2)}) %all-to-all-start.13) | async-done | bytes 1310752 | tf_op jit(solution)/shard_map/all_to_all | solution.py:203
  (840 shorter events, 874.6 us)
Async XLA Ops:
  0.6 13.5 %copy-start = (bf16[128,1,4096]{2,0,1:T(8,128)(2,1)S(1)}, bf16[128,1,4096]{2,0,1:T(8,128)(2,1)}, u32[]{:S(2)}) copy-start(bf16[128,1,4096]{2,0,1:T(8,128)(2,1)} %param.26) | copy-start | bytes 3145732
  5.9 7.7 copy-start.10
  5.9 7.7 copy-start.13
  5.9 30.5 %all-to-all-start.7 = ((bf16[160,1,16,2,128]{4,0,3,1,2:T(8,128)(2,1)}), bf16[160,1,16,2,128]{4,0,3,1,2:T(8,128)(2,1)S(1)}, u32[]{:S(2)}, u32[]{:S(2)}) async-start(bf16[160,1,16,2,128]{4,0,3,1,2:T(8,128)(2,1)} %copy.172), calls=%async_computation.7 | async-start | bytes 2621440 | tf_op jit(solution)/shard_map/all_to_all | solution.py:186
  14.2 2.4 copy-start.2
  16.6 2.4 copy-start.3
  150.7 52.1 %all-to-all-start = ((bf16[10,16,4096]{2,0,1:T(8,128)(2,1)}), bf16[10,16,4096]{2,0,1:T(8,128)(2,1)S(1)}, u32[]{:S(2)}, u32[]{:S(2)}) async-start(bf16[10,16,4096]{2,0,1:T(8,128)(2,1)} %get-tuple-element.1228), calls=%async_computation | async-start | bytes 4194304 | tf_op jit(solution)/shard_map/all_to_all | solution.py:177
  202.8 27.4 %all-to-all-start.3 = ((bf16[160,1,16,2,128]{4,0,3,1,2:T(8,128)(2,1)}), bf16[160,1,16,2,128]{4,0,3,1,2:T(8,128)(2,1)}, u32[]{:S(2)}, u32[]{:S(2)}) async-start(bf16[160,1,16,2,128]{4,0,3,1,2:T(8,128)(2,1)} %copy.162), calls=%async_computation.3 | async-start | bytes 2621440 | tf_op jit(solution)/shard_map/all_to_all | solution.py:184
  230.2 22.2 %all-to-all-start.5 = ((bf16[160,1,16,2,128]{4,0,3,1,2:T(8,128)(2,1)}), bf16[160,1,16,2,128]{4,0,3,1,2:T(8,128)(2,1)}, u32[]{:S(2)}, u32[]{:S(2)}) async-start(bf16[160,1,16,2,128]{4,0,3,1,2:T(8,128)(2,1)} %copy.166), calls=%async_computation.5 | async-start | bytes 2621440 | tf_op jit(solution)/shard_map/all_to_all | solution.py:183
  243.5 16.1 %copy-start.12 = (s32[15]{0:T(128)S(1)}, s32[15]{0:T(128)}, u32[]{:S(2)}) copy-start(s32[15]{0:T(128)} %constant.203) | copy-start | bytes 184
  252.5 135.6 %all-to-all-start.1 = ((bf16[160,1,16,2,128]{4,0,3,1,2:T(8,128)(2,1)}), bf16[160,1,16,2,128]{4,0,3,1,2:T(8,128)(2,1)}, u32[]{:S(2)}, u32[]{:S(2)}) async-start(bf16[160,1,16,2,128]{4,0,3,1,2:T(8,128)(2,1)} %copy.158), calls=%async_computation.1 | async-start | bytes 2621440 | tf_op jit(solution)/shard_map/all_to_all | solution.py:185
  257.6 3.5 copy-start.11
  263.5 263.0 %copy-start.4 = (bf16[160,1,16,2,128]{4,2,0,3,1:T(8,128)(2,1)}, bf16[160,1,16,2,128]{4,2,0,3,1:T(8,128)(2,1)S(1)}, u32[]{:S(2)}) copy-start(bf16[160,1,16,2,128]{4,2,0,3,1:T(8,128)(2,1)S(1)} %copy.173) | copy-start | bytes 3932164
  387.0 1.1 copy-start.8
  390.2 3.5 copy-start.5
  767.8 20.9 %all-to-all-start.8 = ((bf16[160,16,1,2,128]{4,0,3,2,1:T(8,128)(2,1)}), bf16[160,16,1,2,128]{4,0,3,2,1:T(8,128)(2,1)}, u32[]{:S(2)}, u32[]{:S(2)}) async-start(bf16[160,16,1,2,128]{4,0,3,2,1:T(8,128)(2,1)} %copy.175), calls=%async_computation.8 | async-start | bytes 2621440 | tf_op jit(solution)/shard_map/all_to_all | solution.py:193
  788.7 18.5 %all-to-all-start.10 = ((bf16[160,16,1,2,128]{4,0,3,2,1:T(8,128)(2,1)}), bf16[160,16,1,2,128]{4,0,3,2,1:T(8,128)(2,1)}, u32[]{:S(2)}, u32[]{:S(2)}) async-start(bf16[160,16,1,2,128]{4,0,3,2,1:T(8,128)(2,1)} %copy.180), calls=%async_computation.10 | async-start | bytes 2621440 | tf_op jit(solution)/shard_map/all_to_all | solution.py:194
  797.3 13.5 %copy-start.7 = (bf16[2560,2,128]{2,0,1:T(8,128)(2,1)S(1)}, bf16[2560,2,128]{2,0,1:T(8,128)(2,1)}, u32[]{:S(2)}) copy-start(bf16[2560,2,128]{2,0,1:T(8,128)(2,1)} %copy-done.6) | copy-start | bytes 3932164
  807.1 17.7 %all-to-all-start.12 = ((bf16[160,16,1,2,128]{4,0,3,2,1:T(8,128)(2,1)}), bf16[160,16,1,2,128]{4,0,3,2,1:T(8,128)(2,1)S(1)}, u32[]{:S(2)}, u32[]{:S(2)}) async-start(bf16[160,16,1,2,128]{4,0,3,2,1:T(8,128)(2,1)} %copy.185), calls=%async_computation.12 | async-start | bytes 2621440 | tf_op jit(solution)/shard_map/all_to_all | solution.py:195
  825.9 17.7 %all-to-all-start.6 = ((bf16[160,16,1,2,128]{4,3,0,2,1:T(2,128)(2,1)}), bf16[160,16,1,2,128]{4,3,0,2,1:T(2,128)(2,1)S(1)}, u32[]{:S(2)}, u32[]{:S(2)}) async-start(bf16[160,16,1,2,128]{4,3,0,2,1:T(2,128)(2,1)} %copy.170), calls=%async_computation.6 | async-start | bytes 2621440 | tf_op jit(solution)/shard_map/all_to_all | solution.py:192
  843.7 68.5 %all-to-all-start.9 = ((bf16[10,16,4096]{2,0,1:T(8,128)(2,1)}), bf16[10,16,4096]{2,0,1:T(8,128)(2,1)S(1)}, u32[]{:S(2)}, u32[]{:S(2)}) async-start(bf16[10,16,4096]{2,0,1:T(8,128)(2,1)} %copy.177), calls=%async_computation.9 | async-start | bytes 4194304 | tf_op jit(solution)/shard_map/all_to_all | solution.py:201
  912.2 54.0 %all-to-all-start.11 = ((bf16[10,16,4096]{2,0,1:T(8,128)(2,1)}), bf16[10,16,4096]{2,0,1:T(8,128)(2,1)}, u32[]{:S(2)}, u32[]{:S(2)}) async-start(bf16[10,16,4096]{2,0,1:T(8,128)(2,1)} %copy.182), calls=%async_computation.11 | async-start | bytes 4194304 | tf_op jit(solution)/shard_map/all_to_all | solution.py:202
  966.2 54.2 %all-to-all-start.13 = ((bf16[10,16,4096]{2,0,1:T(8,128)(2,1)}), bf16[10,16,4096]{2,0,1:T(8,128)(2,1)}, u32[]{:S(2)}, u32[]{:S(2)}) async-start(bf16[10,16,4096]{2,0,1:T(8,128)(2,1)} %copy.187), calls=%async_computation.13 | async-start | bytes 4194304 | tf_op jit(solution)/shard_map/all_to_all | solution.py:203
  1024.9 3.1 copy-start.1
  (2 other events, 2.1 us)
where the time goes:
time: 1040 us; the launch traced here: 1030 us
  local copies, waits for them, and re-layouts  283 us (27%)
  matrix products  210 us (20%)
  waiting for transfers between devices  204 us (20%)
  blocking collectives  114 us (11%)
  loops' own time  92.3 us (9%)
  starting transfers between devices  76.5 us (7%)
  other arithmetic  46.9 us (5%)
    all_to_all x1, blocking collectives, to_groups(): lax.all_to_all(second_part, 'dp', split_axis=1, concat_axis=1, tiled=True)  60.6 us
    dynamic_slice x45, local copies, waits for them, and re-layouts, tile_scores(): q_start = query_block[pair_index] * block_rows  56.3 us
    dynamic_slice x45, local copies, waits for them, and re-layouts, tile_scores(): k_start = key_block[pair_index] * block_rows  56.3 us
    all_to_all x1, blocking collectives, to_groups(): lax.all_to_all(first_part, 'dp', split_axis=1, concat_axis=1, tiled=True)  53.7 us
    dot_general x30, matrix products, tile_scores(): jnp.einsum('qhe,khe->qhk', q_rows, k_rows, preferred_element_type=jnp.flo...  49.3 us
    dot_general x15, matrix products, value_compute(): jnp.einsum('qhk,khe->qhe', weight, v_rows, preferred_element_type=jnp.flo...  44.9 us
    all_to_all x1, waiting for transfers between devices, to_packed(): lax.all_to_all(second_part, 'dp', split_axis=1, concat_axis=1, tiled=True)  37.9 us
    all_to_all x1, waiting for transfers between devices, to_packed(): lax.all_to_all(first_part, 'dp', split_axis=1, concat_axis=1, tiled=True)  37.7 us
  transfers between devices with their start and end apart: 12, of which 10 were waited for; matrix products, arithmetic and copies ran while one was open for 20% of the time, Pallas kernels for 0%

commit v1 on v0

v1 whole, which is shorter than its diff:
```python
import functools

import jax
import jax.numpy as jnp
import numpy as np
from jax import lax
from jax.experimental import pallas as pl
from jax.experimental.pallas import tpu as pltpu
from jax.sharding import PartitionSpec as P

HEAD = 128
NEGATIVE_FILL = -1e30
LOG2E = 1.4426950408889634
BLOCK = 512
MESH = pl.DeviceIdType.MESH


def group_tables(doc_lengths, doc_group, group_count, per_unit):
    doc_ends = jnp.cumsum(doc_lengths)
    member = (doc_group[:, None] == jnp.arange(group_count, dtype=jnp.int32)[None, :]).astype(
        jnp.int32
    )
    group_units = jnp.sum(member * doc_lengths[:, None], axis=0) // per_unit
    first_unit = jnp.cumsum(group_units) - group_units
    return (doc_ends, group_units, first_unit)


def greet_all(seq, dp, n_seq, n_dp):
    me = seq * n_dp + dp
    total = n_seq * n_dp
    barrier = pltpu.get_barrier_semaphore()

    def greet(offset, carry):
        peer = lax.rem(me + offset, total)
        pl.semaphore_signal(
            barrier, 1, device_id=(peer // n_dp, lax.rem(peer, n_dp)), device_id_type=MESH
        )
        return carry

    lax.fori_loop(1, total, greet, 0)
    pl.semaphore_wait(barrier, total - 1)


def scatter_kernel(n_seq, n_dp, packed, cot, out, send_sem, recv_sem, cot_send, cot_recv):
    seq, dp = lax.axis_index("seq"), lax.axis_index("dp")
    total = n_seq * n_dp
    me = seq * n_dp + dp
    greet_all(seq, dp, n_seq, n_dp)

    def send_cot(offset, carry):
        peer = lax.rem(seq + offset, n_seq)
        pltpu.make_async_remote_copy(
            cot.at[:, :, peer],
            out.at[3, :, pl.ds(seq * n_dp, n_dp)],
            cot_send,
            cot_recv,
            device_id=(peer, dp),
            device_id_type=MESH,
        ).start()
        return carry

    lax.fori_loop(1, n_seq, send_cot, 0)

    def send(offset, carry):
        to_seq = lax.rem(seq + offset // n_dp, n_seq)
        to_dp = lax.rem(dp + lax.rem(offset, n_dp), n_dp)
        pltpu.make_async_remote_copy(
            packed.at[:, to_dp, :, to_seq],
            out.at[pl.ds(0, 3), :, me],
            send_sem,
            recv_sem,
            device_id=(to_seq, to_dp),
            device_id_type=MESH,
        ).start()
        return carry

    lax.fori_loop(1, total, send, 0)
    pltpu.make_async_copy(packed.at[:, dp, :, seq], out.at[pl.ds(0, 3), :, me], recv_sem).start()
    pltpu.make_async_copy(
        cot.at[:, :, seq], out.at[3, :, pl.ds(seq * n_dp, n_dp)], cot_recv
    ).start()
    gone = out.at[pl.ds(0, 3), :, pl.ds(0, total - 1)]
    pltpu.make_async_copy(gone, gone, send_sem).wait()
    gone = out.at[3, :, pl.ds(0, total - n_dp)]
    pltpu.make_async_copy(gone, gone, cot_send).wait()
    here = out.at[pl.ds(0, 3)]
    pltpu.make_async_copy(here, here, recv_sem).wait()
    here = out.at[3]
    pltpu.make_async_copy(here, here, cot_recv).wait()


def gather_kernel(n_seq, n_dp, done, grads, att, send_sem, recv_sem, att_send, att_recv):
    seq, dp = lax.axis_index("seq"), lax.axis_index("dp")
    total = n_seq * n_dp
    me = seq * n_dp + dp
    greet_all(seq, dp, n_seq, n_dp)

    def send_att(offset, carry):
        peer = lax.rem(seq + offset, n_seq)
        pltpu.make_async_remote_copy(
            done.at[0, :, pl.ds(peer * n_dp, n_dp)],
            att.at[:, :, seq],
            att_send,
            att_recv,
            device_id=(peer, dp),
            device_id_type=MESH,
        ).start()
        return carry

    lax.fori_loop(1, n_seq, send_att, 0)

    def send(offset, carry):
        to_seq = lax.rem(seq + offset // n_dp, n_seq)
        to_dp = lax.rem(dp + lax.rem(offset, n_dp), n_dp)
        pltpu.make_async_remote_copy(
            done.at[pl.ds(1, 3), :, to_seq * n_dp + to_dp],
            grads.at[:, dp, :, seq],
            send_sem,
            recv_sem,
            device_id=(to_seq, to_dp),
            device_id_type=MESH,
        ).start()
        return carry

    lax.fori_loop(1, total, send, 0)
    pltpu.make_async_copy(done.at[pl.ds(1, 3), :, me], grads.at[:, dp, :, seq], recv_sem).start()
    pltpu.make_async_copy(
        done.at[0, :, pl.ds(seq * n_dp, n_dp)], att.at[:, :, seq], att_recv
    ).start()
    gone = done.at[pl.ds(0, 3), :, pl.ds(0, total - 1)]
    pltpu.make_async_copy(gone, gone, send_sem).wait()
    gone = done.at[0, :, pl.ds(0, total - n_dp)]
    pltpu.make_async_copy(gone, gone, att_send).wait()
    pltpu.make_async_copy(grads, grads, recv_sem).wait()
    pltpu.make_async_copy(att, att, att_recv).wait()


def scatter(packed, cot, n_seq, n_dp):
    cap = packed.shape[2]
    return pl.pallas_call(
        functools.partial(scatter_kernel, n_seq, n_dp),
        out_shape=jax.ShapeDtypeStruct((4, cap, n_seq * n_dp) + packed.shape[4:], packed.dtype),
        in_specs=[pl.BlockSpec(memory_space=pltpu.VMEM)] * 2,
        out_specs=pl.BlockSpec(memory_space=pltpu.VMEM),
        scratch_shapes=[pltpu.SemaphoreType.DMA] * 4,
        compiler_params=pltpu.CompilerParams(
            collective_id=0, has_side_effects=True, vmem_limit_bytes=40 << 20
        ),
        name="scatter_to_heads",
    )(packed, cot)


def gather(done, n_seq, n_dp):
    cap, tail = done.shape[1], done.shape[3:]
    return pl.pallas_call(
        functools.partial(gather_kernel, n_seq, n_dp),
        out_shape=(
            jax.ShapeDtypeStruct((3, n_dp, cap, n_seq) + tail, done.dtype),
            jax.ShapeDtypeStruct((cap, n_dp, n_seq) + tail, done.dtype),
        ),
        in_specs=[pl.BlockSpec(memory_space=pltpu.VMEM)],
        out_specs=(pl.BlockSpec(memory_space=pltpu.VMEM),) * 2,
        scratch_shapes=[pltpu.SemaphoreType.DMA] * 4,
        compiler_params=pltpu.CompilerParams(
            collective_id=1, has_side_effects=True, vmem_limit_bytes=40 << 20
        ),
        name="gather_from_heads",
    )(done)


def dot(a, b, dim_a, dim_b):
    return lax.dot_general(
        a, b, (((dim_a,), (dim_b,)), ((), ())), preferred_element_type=jnp.float32
    )


def attention_kernel(blocks, first_ref, live_ref, data, start, out, dk_acc, dv_acc):
    size = BLOCK
    scale = HEAD ** (-0.5)
    dk_acc[...] = jnp.zeros_like(dk_acc)
    dv_acc[...] = jnp.zeros_like(dv_acc)
    key_iota = lax.broadcasted_iota(jnp.int32, (size, size), 0)
    query_iota = lax.broadcasted_iota(jnp.int32, (size, size), 1)

    def query_block(i, carry):
        rows = pl.ds(pl.multiple_of(i * size, size), size)
        q = data[0, 0, rows, :]
        do = data[3, 0, rows, :]
        low = start[i]
        first = first_ref[i]

        def tile(j):
            keys = pl.ds(pl.multiple_of(j * size, size), size)
            k = data[1, 0, keys, :]
            v = data[2, 0, keys, :]
            scores = dot(k, q, 1, 1) * (scale * LOG2E)
            allowed = (key_iota >= low - j * size) & (key_iota <= query_iota + (i - j) * size)
            return keys, k, v, scores, allowed

        def forward(j, state):
            top, total, acc = state
            keys, k, v, scores, allowed = tile(j)
            scores = jnp.where(allowed, scores, NEGATIVE_FILL)
            new_top = jnp.maximum(top, jnp.max(scores, axis=0, keepdims=True))
            weight = jnp.where(allowed, jnp.exp2(scores - new_top), 0.0)
            shrink = jnp.exp2(top - new_top)
            total = total * shrink + jnp.sum(weight, axis=0, keepdims=True)
            acc = acc * shrink + dot(v, weight.astype(jnp.bfloat16), 0, 0)
            return new_top, total, acc

        top, total, acc = lax.fori_loop(
            first,
            i + 1,
            forward,
            (
                jnp.full((1, size), NEGATIVE_FILL, jnp.float32),
                jnp.zeros((1, size), jnp.float32),
                jnp.zeros((HEAD, size), jnp.float32),
            ),
        )
        log_total = top + jnp.log2(total)
        attended = jnp.transpose(acc / total).astype(jnp.bfloat16)
        row_ids = i * size + lax.broadcasted_iota(jnp.int32, (size, HEAD), 0)
        attended = jnp.where(row_ids < live_ref[0], attended, jnp.zeros_like(attended))
        out[0, 0, rows, :] = attended
        delta = jnp.sum(
            jnp.transpose(do.astype(jnp.float32) * attended.astype(jnp.float32)),
            axis=0,
            keepdims=True,
        )

        def backward(j, grad_q):
            keys, k, v, scores, allowed = tile(j)
            weight = jnp.where(allowed, jnp.exp2(scores - log_total), 0.0)
            grad_prob = dot(v, do, 1, 1)
            grad_score = (weight * (grad_prob - delta)).astype(jnp.bfloat16)
            dv_acc[keys, :] += dot(weight.astype(jnp.bfloat16), do, 1, 0)
            dk_acc[keys, :] += dot(grad_score, q, 1, 0)
            return grad_q + dot(k, grad_score, 0, 0)

        grad_q = lax.fori_loop(
            first, i + 1, backward, jnp.zeros((HEAD, size), jnp.float32)
        )
        out[1, 0, rows, :] = jnp.transpose(grad_q * scale).astype(jnp.bfloat16)
        return carry

    lax.fori_loop(0, blocks, query_block, 0)

    def finish(i, carry):
        rows = pl.ds(pl.multiple_of(i * size, size), size)
        out[2, 0, rows, :] = (dk_acc[rows, :] * scale).astype(jnp.bfloat16)
        out[3, 0, rows, :] = dv_acc[rows, :].astype(jnp.bfloat16)
        return carry

    lax.fori_loop(0, blocks, finish, 0)


def attend(data, start, live):
    _, heads, rows, width = data.shape
    blocks = rows // BLOCK
    spec = pl.BlockSpec((4, 1, rows, width), lambda h, *_: (0, h, 0, 0))
    return pl.pallas_call(
        functools.partial(attention_kernel, blocks),
        out_shape=jax.ShapeDtypeStruct(data.shape, data.dtype),
        grid_spec=pltpu.PrefetchScalarGridSpec(
            num_scalar_prefetch=2,
            grid=(heads,),
            in_specs=[spec, pl.BlockSpec((blocks, 1, BLOCK), lambda h, *_: (0, 0, 0))],
            out_specs=spec,
            scratch_shapes=[pltpu.VMEM((rows, width), jnp.float32)] * 2,
        ),
        compiler_params=pltpu.CompilerParams(
            dimension_semantics=("arbitrary",), vmem_limit_bytes=60 << 20
        ),
        name="attend_group",
    )(start[::BLOCK] // BLOCK, live, data, start.reshape(blocks, 1, BLOCK))


def body(queries, keys_in, values, grad_out, doc_lengths, doc_group):
    n_seq = lax.axis_size("seq")
    n_dp = lax.axis_size("dp")
    devices = n_seq * n_dp
    local_rows = queries.shape[0]
    features = queries.shape[2]
    local_heads = features // (n_seq * HEAD)
    cap = grad_out.shape[0]
    tail = (n_seq, local_heads, HEAD)
    doc_ends, group_units, first_unit = group_tables(doc_lengths, doc_group, n_dp, devices)
    slots = jnp.arange(cap, dtype=jnp.int32)[None, :]
    source_row = jnp.minimum(first_unit[:, None] + slots, local_rows - 1).reshape(-1)
    row_ids = jnp.arange(local_rows, dtype=jnp.int32)
    row_group = jnp.sum((first_unit + group_units)[None, :] <= row_ids[:, None], axis=1)
    target_row = row_group * cap + row_ids - jnp.take(first_unit, row_group)

    packed = jnp.stack(
        [
            jnp.take(part.reshape(local_rows, features), source_row, axis=0)
            for part in (queries, keys_in, values)
        ]
    )
    arrived = scatter(
        packed.reshape((3, n_dp, cap) + tail), grad_out.reshape((cap, n_dp) + tail), n_seq, n_dp
    )
    rows = cap * devices
    data = jnp.transpose(arrived.reshape(4, rows, local_heads, HEAD), (0, 2, 1, 3))

    group = lax.axis_index("dp")
    base = first_unit[group] * devices
    live = group_units[group] * devices
    local_ids = jnp.arange(rows, dtype=jnp.int32)
    doc_starts = doc_ends - doc_lengths
    begun = doc_starts[None, :] <= (base + local_ids)[:, None]
    start = jnp.max(jnp.where(begun, doc_starts[None, :] - base, 0), axis=1)
    start = jnp.where(local_ids < live, start, local_ids).astype(jnp.int32)
    done = attend(data, start, live.astype(jnp.int32).reshape(1))

    done = jnp.transpose(done, (0, 2, 1, 3)).reshape(4, cap, devices, local_heads, HEAD)
    grads, attended = gather(done, n_seq, n_dp)
    grads = grads.reshape(3, n_dp * cap, features)
    outs = [
        jnp.take(grads[part], target_row, axis=0).reshape(local_rows, 1, features)
        for part in range(3)
    ]
    return (attended.reshape(cap, n_dp, features),) + tuple(outs)


def solution(mesh):
    return jax.shard_map(
        body,
        mesh=mesh,
        in_specs=(
            P(None, ("seq", "dp"), None),
            P(None, ("seq", "dp"), None),
            P(None, ("seq", "dp"), None),
            P(None, ("seq", "dp"), None),
            P(),
            P(),
        ),
        out_specs=(
            P(None, ("seq", "dp"), None),
            P(None, ("seq", "dp"), None),
            P(None, ("seq", "dp"), None),
            P(None, ("seq", "dp"), None),
        ),
        check_vma=False,
    )
```

time: 1040 us -> 376 us (0.36)
  Pallas kernels: 0 us -> 274 us
  local copies, waits for them, and re-layouts: 283 us -> 65.7 us
  matrix products: 210 us -> 0 us
  waiting for transfers between devices: 204 us -> 0 us
  blocking collectives: 114 us -> 0 us
  loops' own time: 92.3 us -> 0 us
  starting transfers between devices: 76.5 us -> 0 us
  other arithmetic: 46.9 us -> 30.5 us
    pallas_call x0 -> x3, Pallas kernels: none -> 274 us  [the longest x1 114 us: gather(): pl.pallas_call(functools.partial(gather_kernel, n_seq, n_dp), out_shape=(...]
    dot_general x105 -> x0, matrix products: 210 us -> none  [the longest x30 49.3 us: tile_scores(): jnp.einsum('qhe,khe->qhk', q_rows, k_rows, preferred_element_type=jnp.flo...]
    all_to_all x12 -> x0, waiting for transfers between devices: 204 us -> none  [the longest x1 37.9 us: to_packed(): lax.all_to_all(second_part, 'dp', split_axis=1, concat_axis=1, tiled=True)]
    dynamic_slice x302 -> x1, local copies, waits for them, and re-layouts: 151 us -> 0.59 us  [body(): live = group_units[group] * devices]
    all_to_all x2 -> x0, blocking collectives: 114 us -> none  [the longest x1 60.6 us: to_groups(): lax.all_to_all(second_part, 'dp', split_axis=1, concat_axis=1, tiled=True)]
    another operation x48 -> x0, loops' own time: 92.3 us -> none  [the longest x15 20.9 us: grad_step(): lax.cond(needed[pair_index], grad_compute, lambda unchanged: unchanged, l...]
    all_to_all x12 -> x0, starting transfers between devices: 76.5 us -> none  [the longest x1 19.6 us: to_packed(): lax.all_to_all(first_part, 'dp', split_axis=1, concat_axis=1, tiled=True)]
    reshape x20 -> x2, local copies, waits for them, and re-layouts: 58 us -> 5.36 us  [the longest x1 3.55 us: body(): grad_out.reshape((cap, n_dp) + tail)]
  transfers between devices with their start and end apart: 12 -> 0, of which waited for: 10 -> 0; matrix products, arithmetic and copies ran while one was open for 20% -> 0% of each run, Pallas kernels for 0% -> 0%
where the time goes in v1:
time: 376 us; the launch traced here: 373 us
  Pallas kernels  274 us (73%)
  local copies, waits for them, and re-layouts  65.7 us (17%)
  other arithmetic  30.5 us (8%)
    pallas_call x1, Pallas kernels, gather(): pl.pallas_call(functools.partial(gather_kernel, n_seq, n_dp), out_shape=(...  114 us
    pallas_call x1, Pallas kernels, scatter(): pl.pallas_call(functools.partial(scatter_kernel, n_seq, n_dp), out_shape=...  107 us
    pallas_call x1, Pallas kernels, attend(): pl.pallas_call(functools.partial(attention_kernel, blocks), out_shape=jax...  53.4 us
    another operation x3, local copies, waits for them, and re-layouts, body(): jnp.stack([jnp.take(part.reshape(local_rows, features), source_row, axis=...  10.5 us
    squeeze x3, local copies, waits for them, and re-layouts, body(): grads[part]  10.1 us
    transpose x1, local copies, waits for them, and re-layouts, body(): jnp.transpose(done, (0, 2, 1, 3))  10.1 us
    and x1, other arithmetic, body(): jnp.take(grads[part], target_row, axis=0).reshape(local_rows, 1, features)  10.1 us
    another operation x1, other arithmetic, body(): jnp.stack([jnp.take(part.reshape(local_rows, features), source_row, axis=...  9.81 us

profile of v1, /device:TPU:1, one launch (start us, length us, event | category | flops | bytes accessed | tf_op | source)
XLA Modules:
  0.0 372.8 jit_solution(633892394772890328)
XLA Ops:
  5.8 10.1 %compare_and_fusion = (pred[128]{0:T(512)(128)(4,1)S(1)}, s32[128]{0:T(128)S(1)}) fusion(s32[]{:T(128)} %bitcast.36, s32[]{:T(128)} %bitcast.35, s32[]{:T(128)} %bitcast.34, s32[]{:T(128)} %bitcast.33, s32[]{:T(128)} %bitcast.32, s32[]{:T(128)} %bitcast.31, s32[]{:T(128)} %bitcast.30, s32[]{:T(128)} %bitcast.29, s32[]{:T(128)} %bitcast.27, s32[]{:T(128)} %bitcast.25, ...), kind=kLoop, calls=%fused_computation.38 | loop fusion | flops 6272 | bytes 1216 | tf_op jit(solution)/shard_map/jit(_take)/and | solution.py:321
  18.9 2.4 gather_fusion.2
  21.3 2.4 gather_fusion.1
  23.8 2.4 gather_fusion
  26.2 4.0 %broadcast_select_fusion.2 = (bf16[160,4096]{1,0:T(8,128)(2,1)}, bf16[160,4096]{1,0:T(8,128)(2,1)}, bf16[160,4096]{1,0:T(8,128)(2,1)S(1)}) fusion(bf16[160,4096]{1,0:T(8,128)(2,1)} %gather_fusion, pred[160]{0:T(512)(128)(4,1)S(1)} %compare_and_fusion.1, bf16[160,4096]{1,0:T(8,128)(2,1)} %gather_fusion.1, bf16[160,4096]{1,0:T(8,128)(2,1)} %gather_fusion.2), kind=kLoop, calls=%fused_computation.9 | loop fusion | flops 1966080 | bytes 7864480 | tf_op jit(solution)/shard_map/jit(_take)/select_n | solution.py:297
  30.2 4.4 %stack.12 = bf16[1,16,10,16,2,128]{5,4,3,2,1,0:T(2,128)(2,1)} reshape(bf16[160,4096]{1,0:T(8,128)(2,1)} %get-tuple-element.39) | data formatting | bytes 2621440 | tf_op jit(solution)/shard_map/stack | solution.py:295
  34.6 4.4 %stack.13 = bf16[1,16,10,16,2,128]{5,4,3,2,1,0:T(2,128)(2,1)} reshape(bf16[160,4096]{1,0:T(8,128)(2,1)} %get-tuple-element.40) | data formatting | bytes 2621440 | tf_op jit(solution)/shard_map/stack | solution.py:295
  40.7 9.8 %pad_maximum_fusion.packed = bf16[3,16,10,16,2,128]{5,4,3,2,1,0:T(2,128)(2,1)} fusion(bf16[1,16,10,16,2,128]{5,4,3,2,1,0:T(2,128)(2,1)} %stack.14, bf16[1,16,10,16,2,128]{5,4,3,2,1,0:T(2,128)(2,1)} %stack.13, bf16[1,16,10,16,2,128]{5,4,3,2,1,0:T(2,128)(2,1)} %stack.12), kind=kLoop, calls=%fused_computation.6 | loop fusion | flops 3932160 | bytes 7864320 | tf_op jit(solution)/shard_map/stack | solution.py:295
  50.5 3.6 reshape.229.cot
  54.1 2.1 copy-done.1
  56.2 107.4 %scatter_to_heads.1 = bf16[4,10,256,2,128]{4,3,2,1,0:T(2,128)(2,1)S(1)} custom-call(bf16[3,16,10,16,2,128]{5,4,3,2,1,0:T(2,128)(2,1)S(1)} %copy-done.1, bf16[10,16,16,2,128]{4,3,2,1,0:T(2,128)(2,1)S(1)} %reshape.229.cot), custom_call_target="tpu_custom_call" | custom-call | tf_op jit(solution)/shard_map/scatter_to_heads/pallas_call | solution.py:140
  163.6 3.7 copy.20
  167.3 53.4 %attend_group.1 = bf16[4,2,2560,128]{3,2,1,0:T(8,128)(2,1)} custom-call(s32[5]{0:T(128)} %and_select_fusion.1.first_ref, s32[1]{0:T(128)} %mul.28.live_ref, bf16[4,2,2560,128]{3,2,1,0:T(8,128)(2,1)} %bitcast.138, s32[5,1,512]{2,1,0:T(1,128)} %compare_select_fusion.start), custom_call_target="tpu_custom_call" | custom-call | tf_op jit(solution)/shard_map/attend_group/pallas_call | solution.py:262
  220.7 10.1 %copy.21 = bf16[4,2560,2,128]{3,2,1,0:T(2,128)(2,1)S(1)} copy(bf16[4,2560,2,128]{3,1,2,0:T(8,128)(2,1)} %bitcast.139) | data formatting | bytes 10485760 | tf_op jit(solution)/shard_map/transpose | solution.py:317
  230.9 113.6 %gather_from_heads.1 = (bf16[3,16,10,16,2,128]{5,4,3,2,1,0:T(2,128)(2,1)S(1)}, bf16[10,16,16,2,128]{4,3,2,1,0:T(2,128)(2,1)S(1)}) custom-call(bf16[4,10,256,2,128]{4,3,2,1,0:T(2,128)(2,1)S(1)} %bitcast.135), custom_call_target="tpu_custom_call" | custom-call | tf_op jit(solution)/shard_map/gather_from_heads/pallas_call | solution.py:155
  344.5 1.9 copy-done.2
  346.4 1.8 reshape.232
  348.2 5.6 %fusion.3 = (bf16[1,16,10,16,2,128]{5,4,3,2,1,0:T(2,128)(2,1)}, bf16[1,16,10,16,2,128]{5,4,3,2,1,0:T(2,128)(2,1)}, bf16[1,16,10,16,2,128]{5,4,3,2,1,0:T(2,128)(2,1)}) fusion(bf16[3,16,10,16,2,128]{5,4,3,2,1,0:T(2,128)(2,1)} %copy-done.2), kind=kLoop, calls=%fused_computation.64 | loop fusion | bytes 7864320 | tf_op jit(solution)/shard_map/slice | solution.py:321
  353.8 3.4 squeeze.13
  358.4 3.4 squeeze.12
  361.7 2.2 gather_fusion.4
  363.9 3.4 squeeze.11
  367.3 2.2 gather_fusion.3
  369.5 3.4 select_bitcast_fusion
  (36 shorter events, 9.8 us)
Async XLA Ops:
  0.6 1.2 copy-start
  18.9 2.4 copy-start.3
  21.3 2.4 copy-start.4
  54.1 2.1 copy-start.1
  344.5 1.9 copy-start.2

commit v2 on v1

--- a/solution.py
+++ b/solution.py
@@ -189,28 +189,29 @@
         low = start[i]
         first = first_ref[i]
 
-        def tile(j):
+        def tile(j, diagonal):
             keys = pl.ds(pl.multiple_of(j * size, size), size)
             k = data[1, 0, keys, :]
             v = data[2, 0, keys, :]
             scores = dot(k, q, 1, 1) * (scale * LOG2E)
-            allowed = (key_iota >= low - j * size) & (key_iota <= query_iota + (i - j) * size)
-            return keys, k, v, scores, allowed
-
-        def forward(j, state):
+            allowed = key_iota >= low - j * size
+            if diagonal:
+                allowed = allowed & (key_iota <= query_iota)
+            return keys, k, v, jnp.where(allowed, scores, NEGATIVE_FILL)
+
+        def forward(j, state, diagonal=False):
             top, total, acc = state
-            keys, k, v, scores, allowed = tile(j)
-            scores = jnp.where(allowed, scores, NEGATIVE_FILL)
+            keys, k, v, scores = tile(j, diagonal)
             new_top = jnp.maximum(top, jnp.max(scores, axis=0, keepdims=True))
-            weight = jnp.where(allowed, jnp.exp2(scores - new_top), 0.0)
+            weight = jnp.exp2(scores - new_top)
             shrink = jnp.exp2(top - new_top)
             total = total * shrink + jnp.sum(weight, axis=0, keepdims=True)
             acc = acc * shrink + dot(v, weight.astype(jnp.bfloat16), 0, 0)
             return new_top, total, acc
 
-        top, total, acc = lax.fori_loop(
+        state = lax.fori_loop(
             first,
-            i + 1,
+            i,
             forward,
             (
                 jnp.full((1, size), NEGATIVE_FILL, jnp.float32),
@@ -218,6 +219,7 @@
                 jnp.zeros((HEAD, size), jnp.float32),
             ),
         )
+        top, total, acc = forward(i, state, True)
         log_total = top + jnp.log2(total)
         attended = jnp.transpose(acc / total).astype(jnp.bfloat16)
         row_ids = i * size + lax.broadcasted_iota(jnp.int32, (size, HEAD), 0)
@@ -229,18 +231,17 @@
             keepdims=True,
         )
 
-        def backward(j, grad_q):
-            keys, k, v, scores, allowed = tile(j)
-            weight = jnp.where(allowed, jnp.exp2(scores - log_total), 0.0)
+        def backward(j, grad_q, diagonal=False):
+            keys, k, v, scores = tile(j, diagonal)
+            weight = jnp.exp2(scores - log_total)
             grad_prob = dot(v, do, 1, 1)
             grad_score = (weight * (grad_prob - delta)).astype(jnp.bfloat16)
             dv_acc[keys, :] += dot(weight.astype(jnp.bfloat16), do, 1, 0)
             dk_acc[keys, :] += dot(grad_score, q, 1, 0)
             return grad_q + dot(k, grad_score, 0, 0)
 
-        grad_q = lax.fori_loop(
-            first, i + 1, backward, jnp.zeros((HEAD, size), jnp.float32)
-        )
+        grad_q = lax.fori_loop(first, i, backward, jnp.zeros((HEAD, size), jnp.float32))
+        grad_q = backward(i, grad_q, True)
         out[1, 0, rows, :] = jnp.transpose(grad_q * scale).astype(jnp.bfloat16)
         return carry
 
@@ -292,11 +293,12 @@
     row_group = jnp.sum((first_unit + group_units)[None, :] <= row_ids[:, None], axis=1)
     target_row = row_group * cap + row_ids - jnp.take(first_unit, row_group)
 
-    packed = jnp.stack(
-        [
-            jnp.take(part.reshape(local_rows, features), source_row, axis=0)
-            for part in (queries, keys_in, values)
-        ]
+    whole = jnp.concatenate(
+        [part.reshape(local_rows, features) for part in (queries, keys_in, values)], axis=0
+    )
+    part_base = jnp.arange(3, dtype=jnp.int32)[:, None]
+    packed = jnp.take(
+        whole, (source_row[None, :] + part_base * local_rows).reshape(-1), axis=0, mode="clip"
     )
     arrived = scatter(
         packed.reshape((3, n_dp, cap) + tail), grad_out.reshape((cap, n_dp) + tail), n_seq, n_dp
@@ -316,9 +318,11 @@
 
     done = jnp.transpose(done, (0, 2, 1, 3)).reshape(4, cap, devices, local_heads, HEAD)
     grads, attended = gather(done, n_seq, n_dp)
-    grads = grads.reshape(3, n_dp * cap, features)
+    grads = grads.reshape(3 * n_dp * cap, features)
     outs = [
-        jnp.take(grads[part], target_row, axis=0).reshape(local_rows, 1, features)
+        jnp.take(grads, target_row + part * n_dp * cap, axis=0, mode="clip").reshape(
+            local_rows, 1, features
+        )
         for part in range(3)
     ]
     return (attended.reshape(cap, n_dp, features),) + tuple(outs)

time: 376 us -> 344 us (0.915)
  other arithmetic: 30.5 us -> 15.1 us
  Pallas kernels: 274 us -> 263 us
    reshape x0 -> x2, local copies, waits for them, and re-layouts: none -> 19.6 us  [the longest x1 10 us: body(): packed.reshape((3, n_dp, cap) + tail)]
    pallas_call x1, Pallas kernels: 114 us -> 101 us  [gather(): pl.pallas_call(functools.partial(gather_kernel, n_seq, n_dp), out_shape=(...]
    another operation x4 -> x1, local copies, waits for them, and re-layouts: 11.3 us -> 0.74 us  [the longest x3 10.5 us: body(): jnp.stack([jnp.take(part.reshape(local_rows, features), source_row, axis=...]
    squeeze x3 -> x0, local copies, waits for them, and re-layouts: 10.1 us -> none  [body(): grads[part]]
    and x2 -> x0, other arithmetic: 10.1 us -> none  [the longest x1 10.1 us: body(): jnp.take(grads[part], target_row, axis=0).reshape(local_rows, 1, features)]
    add x0 -> x3, other arithmetic: none -> 9.91 us  [the longest x2 9.84 us: body(): target_row + part * n_dp * cap]
    another operation x5 -> x4, other arithmetic: 10.1 us -> 0.32 us  [the longest x1 9.81 us: body(): jnp.stack([jnp.take(part.reshape(local_rows, features), source_row, axis=...]
    gather x6 -> x4, local copies, waits for them, and re-layouts: 12.8 us -> 21.7 us  [the longest x3 17.4 us: body(): jnp.take(grads, target_row + part * n_dp * cap, axis=0, mode='clip')]
where the time goes in v2:
time: 344 us
  Pallas kernels  263 us (76%)
  local copies, waits for them, and re-layouts  64.2 us (19%)
  other arithmetic  15.1 us (4%)
    pallas_call x1, Pallas kernels, scatter(): pl.pallas_call(functools.partial(scatter_kernel, n_seq, n_dp), out_shape=...  107 us
    pallas_call x1, Pallas kernels, gather(): pl.pallas_call(functools.partial(gather_kernel, n_seq, n_dp), out_shape=(...  101 us
    pallas_call x1, Pallas kernels, attend(): pl.pallas_call(functools.partial(attention_kernel, blocks), out_shape=jax...  54.4 us
    gather x3, local copies, waits for them, and re-layouts, body(): jnp.take(grads, target_row + part * n_dp * cap, axis=0, mode='clip')  17.4 us
    transpose x1, local copies, waits for them, and re-layouts, body(): jnp.transpose(done, (0, 2, 1, 3))  10.1 us
    reshape x1, local copies, waits for them, and re-layouts, body(): packed.reshape((3, n_dp, cap) + tail)  10 us
    add x2, other arithmetic, body(): target_row + part * n_dp * cap  9.84 us
    reshape x1, local copies, waits for them, and re-layouts, body(): grads = grads.reshape(3 * n_dp * cap, features)  9.6 us

profile of v2, /device:TPU:1, one launch (start us, length us, event | category | flops | bytes accessed | tf_op | source)
XLA Modules:
  0.0 344.1 jit_solution(11299331481844496588)
XLA Ops:
  0.6 0.8 select_reduce_fusion.1
  1.7 0.7 fusion.6
  3.0 0.7 copy.18
  3.9 0.7 broadcast_subtract_fusion
  4.8 0.6 dynamic_slice.6
  6.0 0.6 compare_select_fusion.start
  6.7 0.5 and_select_fusion.1.first_ref
  7.6 2.0 pad_maximum_fusion
  9.6 4.3 %gather_fusion = bf16[480,4096]{1,0:T(8,128)(2,1)} fusion(bf16[384,4096]{1,0:T(8,128)(2,1)S(1)} %pad_maximum_fusion, s32[1024]{0:T(1024)S(1)} %pad_clamp_fusion.3), kind=kCustom, calls=%fused_computation | custom fusion | bytes 7866240 | tf_op jit(solution)/shard_map/jit(_take)/gather | solution.py:300
  13.9 10.0 %reshape.308.packed = bf16[3,16,10,16,2,128]{5,4,3,2,1,0:T(2,128)(2,1)} reshape(bf16[480,4096]{1,0:T(8,128)(2,1)} %gather_fusion) | data formatting | bytes 7864320 | tf_op jit(solution)/shard_map/reshape | solution.py:304
  23.9 0.9 reshape.309.cot
  24.9 2.1 copy-done
  27.0 107.4 %scatter_to_heads.1 = bf16[4,10,256,2,128]{4,3,2,1,0:T(2,128)(2,1)S(1)} custom-call(bf16[3,16,10,16,2,128]{5,4,3,2,1,0:T(2,128)(2,1)S(1)} %copy-done, bf16[10,16,16,2,128]{4,3,2,1,0:T(2,128)(2,1)S(1)} %reshape.309.cot), custom_call_target="tpu_custom_call" | custom-call | tf_op jit(solution)/shard_map/scatter_to_heads/pallas_call | solution.py:140
  134.4 3.7 %copy.20 = bf16[4,10,256,2,128]{4,2,1,3,0:T(8,128)(2,1)} copy(bf16[4,10,256,2,128]{4,3,2,1,0:T(2,128)(2,1)S(1)} %scatter_to_heads.1) | data formatting | bytes 10485760 | tf_op jit(solution)/shard_map/scatter_to_heads/pallas_call | solution.py:140
  138.0 54.4 %attend_group.1 = bf16[4,2,2560,128]{3,2,1,0:T(8,128)(2,1)} custom-call(s32[5]{0:T(128)} %and_select_fusion.1.first_ref, s32[1]{0:T(128)} %mul.51.live_ref, bf16[4,2,2560,128]{3,2,1,0:T(8,128)(2,1)} %bitcast.145, s32[5,1,512]{2,1,0:T(1,128)} %compare_select_fusion.start), custom_call_target="tpu_custom_call" | custom-call | tf_op jit(solution)/shard_map/attend_group/pallas_call | solution.py:263
  192.4 10.1 %copy.21 = bf16[4,2560,2,128]{3,2,1,0:T(2,128)(2,1)S(1)} copy(bf16[4,2560,2,128]{3,1,2,0:T(8,128)(2,1)} %bitcast.146) | data formatting | bytes 10485760 | tf_op jit(solution)/shard_map/transpose | solution.py:319
  202.5 100.9 %gather_from_heads.1 = (bf16[3,16,10,16,2,128]{5,4,3,2,1,0:T(2,128)(2,1)S(1)}, bf16[10,16,16,2,128]{4,3,2,1,0:T(2,128)(2,1)S(1)}) custom-call(bf16[4,10,256,2,128]{4,3,2,1,0:T(2,128)(2,1)S(1)} %bitcast.144), custom_call_target="tpu_custom_call" | custom-call | tf_op jit(solution)/shard_map/gather_from_heads/pallas_call | solution.py:155
  303.5 1.9 copy-done.1
  305.4 9.6 %reshape.313 = bf16[480,4096]{1,0:T(8,128)(2,1)} reshape(bf16[3,16,10,16,2,128]{5,4,3,2,1,0:T(2,128)(2,1)} %copy-done.1) | data formatting | bytes 7864320 | tf_op jit(solution)/shard_map/reshape | solution.py:321
  315.1 9.8 %add_bitcast_fusion = (s32[128]{0:T(128)S(1)}, s32[128,1]{0,1:T(1,128)S(1)}) fusion(s32[]{:T(128)} %bitcast.36, s32[]{:T(128)} %bitcast.35, s32[]{:T(128)} %bitcast.34, s32[]{:T(128)} %bitcast.33, s32[]{:T(128)} %bitcast.32, s32[]{:T(128)} %bitcast.31, s32[]{:T(128)} %bitcast.30, s32[]{:T(128)} %bitcast.29, s32[]{:T(128)} %bitcast.27, s32[]{:T(128)} %bitcast.25, ...), kind=kLoop, calls=%fused_computation.55 | loop fusion | flops 5248 | bytes 1600 | tf_op jit(solution)/shard_map/add | solution.py:323
  324.9 5.8 %gather_fusion.2 = bf16[128,4096]{1,0:T(8,128)(2,1)} fusion(bf16[480,4096]{1,0:T(8,128)(2,1)} %reshape.313, s32[1024]{0:T(1024)S(1)} %pad_clamp_fusion.1), kind=kCustom, calls=%fused_computation.2 | custom fusion | bytes 2097664 | tf_op jit(solution)/shard_map/jit(_take)/gather | solution.py:323
  330.7 5.8 %gather_fusion.1 = bf16[128,4096]{1,0:T(8,128)(2,1)} fusion(bf16[480,4096]{1,0:T(8,128)(2,1)} %reshape.313, s32[1024]{0:T(1024)S(1)} %pad_clamp_fusion.2), kind=kCustom, calls=%fused_computation.1 | custom fusion | bytes 2097664 | tf_op jit(solution)/shard_map/jit(_take)/gather | solution.py:323
  336.5 5.8 %gather_fusion.3 = bf16[128,4096]{1,0:T(8,128)(2,1)} fusion(bf16[480,4096]{1,0:T(8,128)(2,1)} %reshape.313, s32[1024]{0:T(1024)S(1)} %pad_clamp_fusion), kind=kCustom, calls=%fused_computation.3 | custom fusion | bytes 2097664 | tf_op jit(solution)/shard_map/jit(_take)/gather | solution.py:323
  342.3 1.8 reshape.312
  (27 shorter events, 1.1 us)
Async XLA Ops:
  13.9 10.0 %copy-start.2 = (bf16[10,16,4096]{2,1,0:T(8,128)(2,1)S(1)}, bf16[10,16,4096]{2,1,0:T(8,128)(2,1)}, u32[]{:S(2)}) copy-start(bf16[10,16,4096]{2,1,0:T(8,128)(2,1)} %param.9) | copy-start | bytes 3932164
  24.8 2.1 copy-start
  303.5 1.9 copy-start.1

commit v3 on v2

--- a/solution.py
+++ b/solution.py
@@ -144,7 +144,7 @@
         out_specs=pl.BlockSpec(memory_space=pltpu.VMEM),
         scratch_shapes=[pltpu.SemaphoreType.DMA] * 4,
         compiler_params=pltpu.CompilerParams(
-            collective_id=0, has_side_effects=True, vmem_limit_bytes=40 << 20
+            collective_id=0, has_side_effects=True, vmem_limit_bytes=24 << 20
         ),
         name="scatter_to_heads",
     )(packed, cot)
@@ -162,7 +162,7 @@
         out_specs=(pl.BlockSpec(memory_space=pltpu.VMEM),) * 2,
         scratch_shapes=[pltpu.SemaphoreType.DMA] * 4,
         compiler_params=pltpu.CompilerParams(
-            collective_id=1, has_side_effects=True, vmem_limit_bytes=40 << 20
+            collective_id=1, has_side_effects=True, vmem_limit_bytes=24 << 20
         ),
         name="gather_from_heads",
     )(done)
@@ -271,7 +271,7 @@
             scratch_shapes=[pltpu.VMEM((rows, width), jnp.float32)] * 2,
         ),
         compiler_params=pltpu.CompilerParams(
-            dimension_semantics=("arbitrary",), vmem_limit_bytes=60 << 20
+            dimension_semantics=("arbitrary",), vmem_limit_bytes=32 << 20
         ),
         name="attend_group",
     )(start[::BLOCK] // BLOCK, live, data, start.reshape(blocks, 1, BLOCK))
@@ -291,7 +291,9 @@
     source_row = jnp.minimum(first_unit[:, None] + slots, local_rows - 1).reshape(-1)
     row_ids = jnp.arange(local_rows, dtype=jnp.int32)
     row_group = jnp.sum((first_unit + group_units)[None, :] <= row_ids[:, None], axis=1)
-    target_row = row_group * cap + row_ids - jnp.take(first_unit, row_group)
+    group_ids = jnp.arange(n_dp, dtype=jnp.int32)[None, :]
+    shift = jnp.where(group_ids == row_group[:, None], group_ids * cap - first_unit[None, :], 0)
+    target_row = row_ids + jnp.sum(shift, axis=1)
 
     whole = jnp.concatenate(
         [part.reshape(local_rows, features) for part in (queries, keys_in, values)], axis=0

time: 344 us -> 367 us (1.067)
  local copies, waits for them, and re-layouts: 64.2 us -> 101 us
  other arithmetic: 15.1 us -> 4.35 us
  Pallas kernels: 263 us -> 258 us
    transpose x1, local copies, waits for them, and re-layouts: 10.1 us -> 49.8 us  [body(): jnp.transpose(done, (0, 2, 1, 3))]
    add x2 -> x1, other arithmetic: 9.84 us -> 0.01 us  [body(): target_row + part * n_dp * cap]
where the time goes in v3:
time: 367 us; the launch traced here: 366 us
  Pallas kernels  258 us (70%)
  local copies, waits for them, and re-layouts  101 us (28%)
  other arithmetic  4.35 us (1%)
    pallas_call x1, Pallas kernels, scatter(): pl.pallas_call(functools.partial(scatter_kernel, n_seq, n_dp), out_shape=...  107 us
    pallas_call x1, Pallas kernels, gather(): pl.pallas_call(functools.partial(gather_kernel, n_seq, n_dp), out_shape=(...  98.4 us
    pallas_call x1, Pallas kernels, attend(): pl.pallas_call(functools.partial(attention_kernel, blocks), out_shape=jax...  51.8 us
    transpose x1, local copies, waits for them, and re-layouts, body(): jnp.transpose(done, (0, 2, 1, 3))  49.8 us
    gather x3, local copies, waits for them, and re-layouts, body(): jnp.take(grads, target_row + part * n_dp * cap, axis=0, mode='clip')  17.4 us
    reshape x1, local copies, waits for them, and re-layouts, body(): packed.reshape((3, n_dp, cap) + tail)  10 us
    reshape x1, local copies, waits for them, and re-layouts, body(): grads = grads.reshape(3 * n_dp * cap, features)  9.59 us

profile of v3, /device:TPU:1, one launch (start us, length us, event | category | flops | bytes accessed | tf_op | source)
XLA Modules:
  0.0 365.5 jit_solution(11323908544944952320)
XLA Ops:
  0.6 0.8 select_reduce_fusion.2
  1.6 0.1 reduce.1
  1.7 0.6 dynamic_slice.7
  2.9 0.7 copy.18
  3.7 0.1 reduce
  3.8 0.7 broadcast_subtract_fusion
  4.5 0.1 select_reduce_fusion
  4.7 0.6 dynamic_slice.6
  6.4 2.0 pad_maximum_fusion
  8.4 4.3 %gather_fusion = bf16[480,4096]{1,0:T(8,128)(2,1)} fusion(bf16[384,4096]{1,0:T(8,128)(2,1)S(1)} %pad_maximum_fusion, s32[1024]{0:T(1024)S(1)} %pad_clamp_fusion.3), kind=kCustom, calls=%fused_computation | custom fusion | bytes 7866240 | tf_op jit(solution)/shard_map/jit(_take)/gather | solution.py:302
  12.7 10.0 %reshape.290.packed = bf16[3,16,10,16,2,128]{5,4,3,2,1,0:T(2,128)(2,1)} reshape(bf16[480,4096]{1,0:T(8,128)(2,1)} %gather_fusion) | data formatting | bytes 7864320 | tf_op jit(solution)/shard_map/reshape | solution.py:306
  22.8 0.9 reshape.291.cot
  23.7 2.1 copy-done
  25.8 107.4 %scatter_to_heads.1 = bf16[4,10,256,2,128]{4,3,2,1,0:T(2,128)(2,1)S(1)} custom-call(bf16[3,16,10,16,2,128]{5,4,3,2,1,0:T(2,128)(2,1)S(1)} %copy-done, bf16[10,16,16,2,128]{4,3,2,1,0:T(2,128)(2,1)S(1)} %reshape.291.cot), custom_call_target="tpu_custom_call" | custom-call | tf_op jit(solution)/shard_map/scatter_to_heads/pallas_call | solution.py:140
  133.3 1.3 copy.20
  134.6 51.8 %attend_group.1 = bf16[4,2,2560,128]{3,2,1,0:T(8,128)(2,1)S(1)} custom-call(s32[5]{0:T(128)S(1)} %and_select_fusion.first_ref, s32[1]{0:T(128)} %mul.38.live_ref, bf16[4,2,2560,128]{3,2,1,0:T(8,128)(2,1)S(1)} %bitcast.36, s32[5,1,512]{2,1,0:T(1,128)S(1)} %compare_select_fusion.start), custom_call_target="tpu_custom_call" | custom-call | tf_op jit(solution)/shard_map/attend_group/pallas_call | solution.py:263
  186.4 49.8 %copy.21 = bf16[4,2560,2,128]{3,2,1,0:T(2,128)(2,1)S(1)} copy(bf16[4,2560,2,128]{3,1,2,0:T(8,128)(2,1)S(1)} %bitcast.37) | data formatting | bytes 10485760 | tf_op jit(solution)/shard_map/transpose | solution.py:321
  236.3 98.4 %gather_from_heads.1 = (bf16[3,16,10,16,2,128]{5,4,3,2,1,0:T(2,128)(2,1)S(1)}, bf16[10,16,16,2,128]{4,3,2,1,0:T(2,128)(2,1)S(1)}) custom-call(bf16[4,10,256,2,128]{4,3,2,1,0:T(2,128)(2,1)S(1)} %bitcast.38), custom_call_target="tpu_custom_call" | custom-call | tf_op jit(solution)/shard_map/gather_from_heads/pallas_call | solution.py:155
  334.7 1.9 copy-done.1
  336.5 9.6 %reshape.295 = bf16[480,4096]{1,0:T(8,128)(2,1)} reshape(bf16[3,16,10,16,2,128]{5,4,3,2,1,0:T(2,128)(2,1)} %copy-done.1) | data formatting | bytes 7864320 | tf_op jit(solution)/shard_map/reshape | solution.py:323
  346.3 5.8 %gather_fusion.2 = bf16[128,4096]{1,0:T(8,128)(2,1)} fusion(bf16[480,4096]{1,0:T(8,128)(2,1)} %reshape.295, s32[1024]{0:T(1024)S(1)} %get-tuple-element.17), kind=kCustom, calls=%fused_computation.2 | custom fusion | bytes 2097664 | tf_op jit(solution)/shard_map/jit(_take)/gather | solution.py:325
  352.1 5.8 %gather_fusion.3 = bf16[128,4096]{1,0:T(8,128)(2,1)} fusion(bf16[480,4096]{1,0:T(8,128)(2,1)} %reshape.295, s32[1024]{0:T(1024)S(1)} %get-tuple-element.16), kind=kCustom, calls=%fused_computation.3 | custom fusion | bytes 2097664 | tf_op jit(solution)/shard_map/jit(_take)/gather | solution.py:325
  357.9 5.8 %gather_fusion.1 = bf16[128,4096]{1,0:T(8,128)(2,1)} fusion(bf16[480,4096]{1,0:T(8,128)(2,1)} %reshape.295, s32[1024]{0:T(1024)S(1)} %pad_clamp_fusion.2), kind=kCustom, calls=%fused_computation.1 | custom fusion | bytes 2097664 | tf_op jit(solution)/shard_map/jit(_take)/gather | solution.py:325
  363.7 1.8 reshape.294
  (26 shorter events, 0.9 us)
Async XLA Ops:
  12.7 10.0 %copy-start.2 = (bf16[10,16,4096]{2,1,0:T(8,128)(2,1)S(1)}, bf16[10,16,4096]{2,1,0:T(8,128)(2,1)}, u32[]{:S(2)}) copy-start(bf16[10,16,4096]{2,1,0:T(8,128)(2,1)} %param.9) | copy-start | bytes 3932164
  23.7 2.1 copy-start
  334.6 1.9 copy-start.1
